TPU v7x, 256 devices: a whole 4x4x8 slice. The times are simulated.
256 devices in a mesh: leaf: 16 (over y, x), row: 16 (over z, core).
Axes of the slice: x: 4, y: 4, z: 8, core: 2. Of those that a mesh axis runs over, the one named last changes fastest.
Arguments:
- sigma_root: float32 [2048, 2048], P(None, 'row')
- linv_one: bfloat16 [16, 2048, 2048], P('leaf', None, 'row'), as said below
- panel_one: bfloat16 [16, 512, 2048], P('leaf', None, 'row'), may hold values from -1.25 to 1.25
- tiles_one: int32 [16, 4], replicated, may hold values from 0 to 15, as said below
- mask_one: int32 [16, 4, 16], P('leaf', None, 'row'), may hold values 0 or 1
- linv_two: bfloat16 [16, 2048, 2048], P('leaf', None, 'row'), as said below
- panel_two: bfloat16 [16, 512, 2048], P('leaf', None, 'row'), may hold values from -1.25 to 1.25
- tiles_two: int32 [16, 4], replicated, may hold values from 0 to 15, as said below
- mask_two: int32 [16, 4, 16], P('leaf', None, 'row'), may hold values 0 or 1
- parent: int32 [16], replicated, may hold values from 0 to 15
Outputs:
- sigma_one: float32 [16, 2048, 2048], P('leaf', None, 'row')
- cross_one: float32 [16, 512, 2048], P('leaf', None, 'row')
- sigma_two: float32 [16, 2048, 2048], P('leaf', None, 'row')
- cross_two: float32 [16, 512, 2048], P('leaf', None, 'row')
Inputs may be any that keep to these rules, and one draw needn't show every extreme that they name: `tiles_one`: each row holds 4 different tile numbers in increasing order. `tiles_two`: each row holds 4 different tile numbers in increasing order. `linv_one`: each block is lower triangular with a positive diagonal. `sigma_root`: symmetric. `linv_two`: each block is lower triangular with a positive diagonal.
All inputs are finite; a program needn't handle non-finite values. No bound on the sum of `mask_one` or of `mask_two` on one device may be relied on, other than what follows from the above.
Results may differ from a plain program's by a relative error of at most 0.00045.
Values may be sent and summed in bfloat16 or wider, within the bound.
No kernel may reach another device: no remote copies, remote signals or barrier semaphores. Data moves between devices by JAX's collectives and lax.ppermute only.
A program may use at most 64 MiB of HBM per device.

v0:
```python
import jax
import jax.numpy as jnp
from jax import lax
from jax.sharding import PartitionSpec as P

TILE = 128


def pattern_rows(tile_list):
    offsets = jnp.arange(TILE, dtype=jnp.int32)
    return (tile_list[..., None] * TILE + offsets).reshape(tile_list.shape[:-1] + (-1,))


def expand_mask(tile_mask):
    return jnp.repeat(jnp.repeat(tile_mask, TILE, axis=0), TILE, axis=1)


def assemble(selected, row_list):
    gathered = lax.all_gather(selected, "row", axis=1, tiled=True)
    return jnp.take(gathered, row_list, axis=1)


def solve_block(selected, row_list, linv_local, panel_local, mask_local):
    select = assemble(selected, row_list)
    masked = panel_local * expand_mask(mask_local).astype(jnp.bfloat16)
    linv_wide = linv_local.astype(jnp.float32)
    whole_panel = lax.all_gather(masked, "row", axis=1, tiled=True)
    upper_part = jnp.dot(whole_panel, linv_local, preferred_element_type=jnp.float32)
    cross = -jnp.dot(select, upper_part, precision=lax.Precision.HIGHEST)
    middle = linv_wide - jnp.dot(
        whole_panel.astype(jnp.float32).T, cross, precision=lax.Precision.HIGHEST
    )
    sigma = jnp.dot(
        lax.all_gather(linv_local, "row", axis=1, tiled=True).astype(jnp.float32).T,
        middle,
        precision=lax.Precision.HIGHEST,
    )
    return (sigma, cross)


def body(
    sigma_root,
    linv_one,
    panel_one,
    tiles_one,
    mask_one,
    linv_two,
    panel_two,
    tiles_two,
    mask_two,
    parent,
):
    leaf_id = lax.axis_index("leaf")
    width = sigma_root.shape[1]
    own_tiles = lax.dynamic_index_in_dim(tiles_one, leaf_id, 0, keepdims=False)
    rows_first = pattern_rows(own_tiles)
    selected_first = jnp.take(sigma_root, rows_first, axis=0)
    sigma_first, cross_first = solve_block(
        selected_first, rows_first, linv_one[0], panel_one[0], mask_one[0]
    )
    rows_every = pattern_rows(tiles_two)
    count = rows_every.shape[0]
    block_rows = rows_every.shape[1]
    owned = (parent == leaf_id).astype(jnp.float32)
    slots = jnp.take(sigma_first, rows_every.reshape(-1), axis=0).reshape(count, block_rows, width)
    slots = slots * owned[:, None, None]
    arrived = lax.all_to_all(slots, "leaf", split_axis=0, concat_axis=0, tiled=True)
    selected_second = jnp.sum(arrived, axis=0)
    rows_second = lax.dynamic_index_in_dim(rows_every, leaf_id, 0, keepdims=False)
    sigma_second, cross_second = solve_block(
        selected_second, rows_second, linv_two[0], panel_two[0], mask_two[0]
    )
    return (sigma_first[None], cross_first[None], sigma_second[None], cross_second[None])


def solution(mesh):
    return jax.shard_map(
        body,
        mesh=mesh,
        in_specs=(
            P(None, "row"),
            P("leaf", None, "row"),
            P("leaf", None, "row"),
            P(),
            P("leaf", None, "row"),
            P("leaf", None, "row"),
            P("leaf", None, "row"),
            P(),
            P("leaf", None, "row"),
            P(),
        ),
        out_specs=(
            P("leaf", None, "row"),
            P("leaf", None, "row"),
            P("leaf", None, "row"),
            P("leaf", None, "row"),
        ),
        check_vma=False,
    )
```

profile of v0, /device:TPU:1, one launch (start us, length us, event | category | flops | bytes accessed | tf_op | source)
XLA Modules:
  0.0 404.3 jit_solution(16791441184361963141)
XLA Ops:
  8.1 1.7 bitcast_multiply_fusion.1
  16.1 39.5 %all-gather.9.cloned.1.call-done = bf16[512,2048]{1,0:T(8,128)(2,1)} async-done(((bf16[512,128]{1,0:T(8,128)(2,1)}), bf16[512,2048]{1,0:T(8,128)(2,1)}) %all-gather.9.cloned.1.call-update) | async-done | bytes 2097168 | tf_op jit(solution)/shard_map/all_gather | solution.py:27
  55.5 2.3 fusion.13
  57.8 48.6 %all-gather.11.cloned.1.call-done = f32[512,2048]{1,0:T(8,128)} async-done(((f32[512,128]{1,0:T(8,128)}), f32[512,2048]{1,0:T(8,128)}) %all-gather.11.cloned.1.call-update) | async-done | bytes 4194320 | tf_op jit(solution)/shard_map/all_gather | solution.py:19
  106.5 5.3 %copy.19 = f32[512,2048]{0,1:T(8,128)} copy(f32[512,2048]{1,0:T(8,128)} %all-gather.11.cloned.1.call-done) | data formatting | bytes 8388608 | tf_op jit(solution)/shard_map/all_gather | solution.py:19
  111.8 4.2 %gather_fusion.2 = f32[512,512]{1,0:T(8,128)S(1)} fusion(f32[512,2048]{0,1:T(8,128)} %copy.19, s32[1024]{0:T(1024)S(1)} %pad_clamp_fusion.1), kind=kCustom, calls=%fused_computation.clone | custom fusion | bytes 2099200 | tf_op jit(solution)/shard_map/jit(_take)/gather | solution.py:20
  116.0 1.9 convolution_negate_fusion.1
  118.6 3.9 convolution_subtract_fusion.1
  122.6 50.3 %all-gather.17.cloned.1.call-done = bf16[1,2048,2048]{2,1,0:T(8,128)(2,1)} async-done(((bf16[1,2048,128]{2,1,0:T(8,128)(2,1)}), bf16[1,2048,2048]{2,1,0:T(8,128)(2,1)}) %all-gather.17.cloned.1.call-update) | async-done | bytes 8388624 | tf_op jit(solution)/shard_map/all_gather | solution.py:34
  172.9 6.3 %fusion.2 = f32[128,2048]{1,0:T(8,128)S(1)} fusion(f32[2048,128]{1,0:T(8,128)S(1)} %convolution_subtract_fusion.1, bf16[1,2048,2048]{2,1,0:T(8,128)(2,1)} %all-gather.17.cloned.1.call-done), kind=kOutput, calls=%fused_computation.6 | convolution fusion | flops 6442450944 | bytes 10485760 | tf_op jit(solution)/shard_map/dot_general | solution.py:33
  179.5 27.8 %gather_fusion.1 = f32[8192,128]{1,0:T(8,128)} fusion(f32[2048,128]{1,0:T(8,128)S(1)} %copy.21, s32[8192]{0:T(1024)S(1)} %broadcast_clamp_fusion), kind=kCustom, calls=%fused_computation.3 | custom fusion | bytes 8421376 | tf_op jit(solution)/shard_map/jit(_take)/gather | solution.py:65
  207.3 5.3 %select_multiply_fusion = f32[16,512,128]{2,1,0:T(8,128)} fusion(f32[16,512,128]{2,1,0:T(8,128)} %bitcast.84, f32[16]{0:T(128)S(1)} %compare_convert_fusion, pred[16,512]{1,0:T(8,128)(4,1)S(1)} %compare_and_fusion), kind=kLoop, calls=%fused_computation.8 | loop fusion | flops 2097152 | bytes 8396864 | tf_op jit(solution)/shard_map/mul | solution.py:66
  212.5 4.7 %all-to-all-start = ((f32[16,512,128]{2,1,0:T(8,128)}), f32[16,512,128]{2,1,0:T(8,128)}, u32[]{:S(2)}, u32[]{:S(2)}) async-start(f32[16,512,128]{2,1,0:T(8,128)} %select_multiply_fusion), calls=%async_computation | async-start | bytes 8388608 | tf_op jit(solution)/shard_map/all_to_all | solution.py:67
  218.2 62.3 %all-to-all-done = f32[16,512,128]{2,1,0:T(8,128)} async-done(((f32[16,512,128]{2,1,0:T(8,128)}), f32[16,512,128]{2,1,0:T(8,128)}, u32[]{:S(2)}, u32[]{:S(2)}) %all-to-all-start) | async-done | bytes 4194336 | tf_op jit(solution)/shard_map/all_to_all | solution.py:67
  280.5 2.4 reduce_sum.9
  284.4 2.3 fusion.11
  286.7 1.3 copy.23
  288.0 35.5 %all-gather.15.cloned.1.call-done = f32[512,2048]{0,1:T(8,128)} async-done(((f32[512,128]{0,1:T(8,128)}), f32[512,2048]{0,1:T(8,128)}) %all-gather.15.cloned.1.call-update) | async-done | bytes 4194320 | tf_op jit(solution)/shard_map/all_gather | solution.py:19
  323.6 4.2 %gather_fusion.3 = f32[512,512]{1,0:T(8,128)S(1)} fusion(f32[512,2048]{0,1:T(8,128)} %all-gather.15.cloned.1.call-done, s32[1024]{0:T(1024)S(1)} %pad_clamp_fusion), kind=kCustom, calls=%fused_computation.1.clone | custom fusion | bytes 2099200 | tf_op jit(solution)/shard_map/jit(_take)/gather | solution.py:20
  327.8 1.9 convolution_negate_fusion
  329.7 4.0 convolution_subtract_fusion
  333.7 56.2 %all-gather.19.cloned.1.call-done = bf16[1,2048,2048]{2,1,0:T(8,128)(2,1)} async-done(((bf16[1,2048,128]{2,1,0:T(8,128)(2,1)}), bf16[1,2048,2048]{2,1,0:T(8,128)(2,1)}) %all-gather.19.cloned.1.call-update) | async-done | bytes 8388624 | tf_op jit(solution)/shard_map/all_gather | solution.py:34
  389.9 6.3 %fusion.4 = f32[1,2048,128]{1,2,0:T(8,128)S(1)} fusion(f32[2048,128]{1,0:T(8,128)S(1)} %convolution_subtract_fusion, bf16[1,2048,2048]{2,1,0:T(8,128)(2,1)} %all-gather.19.cloned.1.call-done), kind=kOutput, calls=%fused_computation.9 | convolution fusion | flops 6442450944 | bytes 10485760 | tf_op jit(solution)/shard_map/dot_general | solution.py:33
  396.2 1.3 copy.24
  (58 shorter events, 10.5 us)
Async XLA Ops:
  7.2 3.6 copy-start
  7.2 48.4 %copy-start.1 = (bf16[1,2048,128]{2,1,0:T(8,128)(2,1)S(1)}, bf16[1,2048,128]{2,1,0:T(8,128)(2,1)}, u32[]{:S(2)}) copy-start(bf16[1,2048,128]{2,1,0:T(8,128)(2,1)} %param.13) | copy-start | bytes 1572868
  7.2 48.3 %all-gather.9.cloned.1.call-start = ((), (), s32[]{:S(2)}) async-start(), calls=%async_computation.1 | async-start | bytes 2228224 | tf_op jit(solution)/shard_map/all_gather | solution.py:27
  9.8 96.7 %all-gather.11.cloned.1.call-start = ((), (), s32[]{:S(2)}) async-start(), calls=%async_computation.2 | async-start | bytes 4456448 | tf_op jit(solution)/shard_map/all_gather | solution.py:19
  12.8 160.1 %all-gather.17.cloned.1.call-start = ((), (), s32[]{:S(2)}) async-start(), calls=%async_computation.5 | async-start | bytes 8912896 | tf_op jit(solution)/shard_map/all_gather | solution.py:34
  117.9 0.7 copy-start.4
  212.5 4.8 %copy-start.6 = (bf16[1,512,128]{2,1,0:T(8,128)(2,1)S(1)}, bf16[1,512,128]{2,1,0:T(8,128)(2,1)}, u32[]{:S(2)}) copy-start(bf16[1,512,128]{2,1,0:T(8,128)(2,1)} %param.18) | copy-start | bytes 393220
  212.5 67.9 %all-to-all-start = ((f32[16,512,128]{2,1,0:T(8,128)}), f32[16,512,128]{2,1,0:T(8,128)}, u32[]{:S(2)}, u32[]{:S(2)}) async-start(f32[16,512,128]{2,1,0:T(8,128)} %select_multiply_fusion), calls=%async_computation | async-start | bytes 8388608 | tf_op jit(solution)/shard_map/all_to_all | solution.py:67
  217.2 67.2 %copy-start.2 = (bf16[1,2048,128]{2,1,0:T(8,128)(2,1)S(1)}, bf16[1,2048,128]{2,1,0:T(8,128)(2,1)}, u32[]{:S(2)}) copy-start(bf16[1,2048,128]{2,1,0:T(8,128)(2,1)} %param.17) | copy-start | bytes 1572868
  217.2 67.2 %all-gather.13.cloned.1.call-start = ((), (), s32[]{:S(2)}) async-start(), calls=%async_computation.3 | async-start | bytes 2228224 | tf_op jit(solution)/shard_map/all_gather | solution.py:27
  218.1 105.4 %all-gather.15.cloned.1.call-start = ((), (), s32[]{:S(2)}) async-start(), calls=%async_computation.4 | async-start | bytes 4456448 | tf_op jit(solution)/shard_map/all_gather | solution.py:19
  283.7 106.2 %all-gather.19.cloned.1.call-start = ((), (), s32[]{:S(2)}) async-start(), calls=%async_computation.6 | async-start | bytes 8912896 | tf_op jit(solution)/shard_map/all_gather | solution.py:34
  288.0 41.6 %copy-start.3 = (bf16[1,2048,128]{2,1,0:T(8,128)(2,1)S(1)}, bf16[1,2048,128]{2,1,0:T(8,128)(2,1)}, u32[]{:S(2)}) copy-start(bf16[1,2048,128]{2,1,0:T(8,128)(2,1)} %param.17) | copy-start | bytes 1572868
  329.7 4.0 copy-start.5
Sparse Core Ops, SparseCore 0:
  10.4 45.1 all-gather.8
  57.9 48.5 all-gather.10
  108.2 64.6 all-gather.16
  220.1 40.0 all-gather.12
  283.9 39.6 all-gather.14
  325.2 64.6 all-gather.18
where the time goes:
time: 405 us; the launch traced here: 404 us
  waiting for transfers between devices  294 us (73%)
  local copies, waits for them, and re-layouts  47.4 us (12%)
  matrix products  28.8 us (7%)
  other arithmetic  15.1 us (4%)
  between operations  14.4 us (4%)
  starting transfers between devices  5.12 us (1%)
    all_gather x2, waiting for transfers between devices, solve_block(): lax.all_gather(linv_local, 'row', axis=1, tiled=True).astype(jnp.float32)  107 us
    all_gather x2, waiting for transfers between devices, assemble(): gathered = lax.all_gather(selected, 'row', axis=1, tiled=True)  84.1 us
    all_to_all x1, waiting for transfers between devices, body(): lax.all_to_all(slots, 'leaf', split_axis=0, concat_axis=0, tiled=True)  62.3 us
    all_gather x2, waiting for transfers between devices, solve_block(): whole_panel = lax.all_gather(masked, 'row', axis=1, tiled=True)  39.5 us
    gather x1, local copies, waits for them, and re-layouts, body(): jnp.take(sigma_first, rows_every.reshape(-1), axis=0)  27.8 us
    dot_general x2, matrix products, solve_block(): jnp.dot(lax.all_gather(linv_local, 'row', axis=1, tiled=True).astype(jnp....  12.5 us
    gather x2, local copies, waits for them, and re-layouts, assemble(): return jnp.take(gathered, row_list, axis=1)  8.43 us
  transfers between devices with their start and end apart: 7, of which 6 were waited for; matrix products, arithmetic and copies ran while one was open for 10% of the time, Pallas kernels for 0%

commit v1 on v0

--- a/solution.py
+++ b/solution.py
@@ -31,7 +31,12 @@
         whole_panel.astype(jnp.float32).T, cross, precision=lax.Precision.HIGHEST
     )
     sigma = jnp.dot(
-        lax.all_gather(linv_local, "row", axis=1, tiled=True).astype(jnp.float32).T,
+        jnp.concatenate(
+            lax.all_to_all(jnp.stack(lax.axis_size("row") * [linv_local], axis=0), "row", 0, 0),
+            axis=1,
+        )
+        .astype(jnp.float32)
+        .T,
         middle,
         precision=lax.Precision.HIGHEST,
     )

time: 405 us -> 623 us (1.54)
  waiting for transfers between devices: 294 us -> 476 us
  starting transfers between devices: 5.12 us -> 23.4 us
  local copies, waits for them, and re-layouts: 47.4 us -> 58.7 us
  matrix products: 28.8 us -> 40 us
    all_gather x2, waiting for transfers between devices: 39.5 us -> 187 us  [solve_block(): whole_panel = lax.all_gather(masked, 'row', axis=1, tiled=True)]
    all_gather x2, waiting for transfers between devices: 84.1 us -> 225 us  [assemble(): gathered = lax.all_gather(selected, 'row', axis=1, tiled=True)]
    all_gather x2 -> x0, waiting for transfers between devices: 107 us -> none  [solve_block(): lax.all_gather(linv_local, 'row', axis=1, tiled=True).astype(jnp.float32)]
    all_to_all x0 -> x2, starting transfers between devices: none -> 16.3 us  [solve_block(): lax.all_to_all(jnp.stack(lax.axis_size('row') * [linv_local], axis=0), 'r...]
    dot_general x2, matrix products: 12.5 us -> 22.6 us  [solve_block(): jnp.dot(jnp.concatenate(lax.all_to_all(jnp.stack(lax.axis_size('row') * [...]
    another operation x0 -> x2, local copies, waits for them, and re-layouts: none -> 8.6 us  [solve_block(): jnp.stack(lax.axis_size('row') * [linv_local], axis=0)]
  transfers between devices with their start and end apart: 7 -> 7, of which waited for: 6 -> 5; matrix products, arithmetic and copies ran while one was open for 10% -> 7% of each run, Pallas kernels for 0% -> 0%
where the time goes in v1:
time: 623 us; the launch traced here: 622 us
  waiting for transfers between devices  476 us (76%)
  local copies, waits for them, and re-layouts  58.7 us (9%)
  matrix products  40 us (6%)
  starting transfers between devices  23.4 us (4%)
  between operations  14.1 us (2%)
  other arithmetic  10.7 us (2%)
    all_gather x2, waiting for transfers between devices, assemble(): gathered = lax.all_gather(selected, 'row', axis=1, tiled=True)  225 us
    all_gather x2, waiting for transfers between devices, solve_block(): whole_panel = lax.all_gather(masked, 'row', axis=1, tiled=True)  187 us
    all_to_all x1, waiting for transfers between devices, body(): lax.all_to_all(slots, 'leaf', split_axis=0, concat_axis=0, tiled=True)  62.7 us
    gather x1, local copies, waits for them, and re-layouts, body(): jnp.take(sigma_first, rows_every.reshape(-1), axis=0)  27.9 us
    dot_general x2, matrix products, solve_block(): jnp.dot(jnp.concatenate(lax.all_to_all(jnp.stack(lax.axis_size('row') * [...  22.6 us
    all_to_all x2, starting transfers between devices, solve_block(): lax.all_to_all(jnp.stack(lax.axis_size('row') * [linv_local], axis=0), 'r...  16.3 us
  transfers between devices with their start and end apart: 7, of which 5 were waited for; matrix products, arithmetic and copies ran while one was open for 7% of the time, Pallas kernels for 0%

profile of v1, /device:TPU:1, one launch (start us, length us, event | category | flops | bytes accessed | tf_op | source)
XLA Modules:
  0.0 622.5 jit_solution(9794216454329186069)
XLA Ops:
  8.5 4.3 stack.6
  12.9 10.1 %all-to-all-start = ((bf16[16,2048,128]{1,2,0:T(8,128)(2,1)}), bf16[16,2048,128]{1,2,0:T(8,128)(2,1)}, u32[]{:S(2)}, u32[]{:S(2)}) async-start(bf16[16,2048,128]{1,2,0:T(8,128)(2,1)} %stack.6), calls=%async_computation | async-start | bytes 16777216 | tf_op jit(solution)/shard_map/all_to_all | solution.py:35
  26.8 94.2 %all-gather.5.cloned.1.call-done = bf16[512,2048]{1,0:T(8,128)(2,1)} async-done(((bf16[512,128]{1,0:T(8,128)(2,1)}), bf16[512,2048]{1,0:T(8,128)(2,1)}) %all-gather.5.cloned.1.call-update) | async-done | bytes 2097168 | tf_op jit(solution)/shard_map/all_gather | solution.py:27
  121.0 2.3 fusion.10
  123.3 116.3 %all-gather.7.cloned.1.call-done = f32[512,2048]{1,0:T(8,128)} async-done(((f32[512,128]{1,0:T(8,128)}), f32[512,2048]{1,0:T(8,128)}) %all-gather.7.cloned.1.call-update) | async-done | bytes 4194320 | tf_op jit(solution)/shard_map/all_gather | solution.py:19
  239.6 5.5 copy.26
  245.0 5.1 gather_fusion.2
  250.1 3.1 convolution_negate_fusion.1
  253.2 3.3 convolution_subtract_fusion.1
  256.5 11.3 %fusion.14 = f32[128,2048]{1,0:T(8,128)S(1)} fusion(f32[2048,128]{1,0:T(8,128)} %convolution_subtract_fusion.1, bf16[2048,2048]{0,1:T(8,128)(2,1)} %bitcast.10), kind=kOutput, calls=%fused_computation.53 | convolution fusion | flops 6442450944 | bytes 10485760 | tf_op jit(solution)/shard_map/dot_general | solution.py:33
  268.1 27.9 %gather_fusion.1 = f32[8192,128]{1,0:T(8,128)} fusion(f32[2048,128]{1,0:T(8,128)S(1)} %copy.29, s32[8192]{0:T(1024)S(1)} %broadcast_clamp_fusion), kind=kCustom, calls=%fused_computation.3 | custom fusion | bytes 8421376 | tf_op jit(solution)/shard_map/jit(_take)/gather | solution.py:70
  296.1 5.3 select_multiply_fusion
  301.3 6.9 %all-to-all-start.1 = ((f32[16,512,128]{2,1,0:T(8,128)}), f32[16,512,128]{2,1,0:T(8,128)}, u32[]{:S(2)}, u32[]{:S(2)}) async-start(f32[16,512,128]{2,1,0:T(8,128)} %select_multiply_fusion), calls=%async_computation.1 | async-start | bytes 8388608 | tf_op jit(solution)/shard_map/all_to_all | solution.py:72
  308.5 62.7 %all-to-all-done.1 = f32[16,512,128]{2,1,0:T(8,128)} async-done(((f32[16,512,128]{2,1,0:T(8,128)}), f32[16,512,128]{2,1,0:T(8,128)}, u32[]{:S(2)}, u32[]{:S(2)}) %all-to-all-start.1) | async-done | bytes 4194336 | tf_op jit(solution)/shard_map/all_to_all | solution.py:72
  371.2 4.3 stack.7
  375.5 6.2 all-to-all-start.2
  382.6 2.4 reduce_sum.9
  386.0 93.2 %all-gather.9.cloned.1.call-done = bf16[512,2048]{1,0:T(8,128)(2,1)} async-done(((bf16[512,128]{1,0:T(8,128)(2,1)}), bf16[512,2048]{1,0:T(8,128)(2,1)}) %all-gather.9.cloned.1.call-update) | async-done | bytes 2097168 | tf_op jit(solution)/shard_map/all_gather | solution.py:27
  479.2 2.3 fusion.8
  482.8 109.2 %all-gather.11.cloned.1.call-done = f32[512,2048]{0,1:T(8,128)} async-done(((f32[512,128]{0,1:T(8,128)}), f32[512,2048]{0,1:T(8,128)}) %all-gather.11.cloned.1.call-update) | async-done | bytes 4194320 | tf_op jit(solution)/shard_map/all_gather | solution.py:19
  591.9 4.9 gather_fusion.3
  596.8 3.1 convolution_negate_fusion
  600.0 3.3 convolution_subtract_fusion
  603.3 11.4 %convolution_bitcast_fusion = f32[1,2048,128]{1,2,0:T(8,128)S(1)} fusion(f32[2048,128]{1,0:T(8,128)} %convolution_subtract_fusion, bf16[2048,2048]{0,1:T(8,128)(2,1)} %bitcast.24), kind=kOutput, calls=%fused_computation.5 | convolution fusion | flops 6442450944 | bytes 10485760 | tf_op jit(solution)/shard_map/dot_general | solution.py:33
  (78 shorter events, 10.0 us)
Async XLA Ops:
  7.2 17.1 %copy-start = (f32[2048,128]{1,0:T(8,128)S(1)}, f32[2048,128]{1,0:T(8,128)}, u32[]{:S(2)}) copy-start(f32[2048,128]{1,0:T(8,128)} %param.12) | copy-start | bytes 3145732
  12.8 10.2 %copy-start.13 = (s32[1,4,1]{1,2,0:T(1,128)S(1)}, s32[1,4,1]{1,2,0:T(1,128)}, u32[]{:S(2)}) copy-start(s32[1,4,1]{1,2,0:T(1,128)} %param.16) | copy-start | bytes 52
  12.8 10.3 %copy-start.9 = (bf16[1,512,128]{2,1,0:T(8,128)(2,1)S(1)}, bf16[1,512,128]{2,1,0:T(8,128)(2,1)}, u32[]{:S(2)}) copy-start(bf16[1,512,128]{2,1,0:T(8,128)(2,1)} %param.14) | copy-start | bytes 393220
  12.8 11.2 %copy-start.11 = (s32[16,4]{0,1:T(4,128)S(1)}, s32[16,4]{0,1:T(4,128)}, u32[]{:S(2)}) copy-start(s32[16,4]{0,1:T(4,128)} %param.15) | copy-start | bytes 772
  12.8 13.5 %copy-start.12 = (s32[16,4]{0,1:T(4,128)S(1)}, s32[16,4]{0,1:T(4,128)}, u32[]{:S(2)}) copy-start(s32[16,4]{0,1:T(4,128)} %param.19) | copy-start | bytes 772
  12.8 13.6 %copy-start.14 = (s32[16]{0:T(128)S(1)}, s32[16]{0:T(128)}, u32[]{:S(2)}) copy-start(s32[16]{0:T(128)} %param.21) | copy-start | bytes 196
  12.9 108.1 %copy-start.4 = (bf16[1,2048,128]{2,1,0:T(8,128)(2,1)S(1)}, bf16[1,2048,128]{2,1,0:T(8,128)(2,1)}, u32[]{:S(2)}) copy-start(bf16[1,2048,128]{2,1,0:T(8,128)(2,1)} %param.13) | copy-start | bytes 1572868
  12.9 243.6 %all-to-all-start = ((bf16[16,2048,128]{1,2,0:T(8,128)(2,1)}), bf16[16,2048,128]{1,2,0:T(8,128)(2,1)}, u32[]{:S(2)}, u32[]{:S(2)}) async-start(bf16[16,2048,128]{1,2,0:T(8,128)(2,1)} %stack.6), calls=%async_computation | async-start | bytes 16777216 | tf_op jit(solution)/shard_map/all_to_all | solution.py:35
  23.0 98.0 %all-gather.5.cloned.1.call-start = ((), (), s32[]{:S(2)}) async-start(), calls=%async_computation.3 | async-start | bytes 2228224 | tf_op jit(solution)/shard_map/all_gather | solution.py:27
  24.0 215.6 %all-gather.7.cloned.1.call-start = ((), (), s32[]{:S(2)}) async-start(), calls=%async_computation.4 | async-start | bytes 4456448 | tf_op jit(solution)/shard_map/all_gather | solution.py:19
  245.0 8.2 %copy-start.2 = (bf16[512,2048]{1,0:T(8,128)(2,1)S(1)}, bf16[512,2048]{1,0:T(8,128)(2,1)}, u32[]{:S(2)}) copy-start(bf16[512,2048]{1,0:T(8,128)(2,1)} %all-gather.5.cloned.1.call-done) | copy-start | bytes 6291460
  245.0 8.2 %copy-start.5 = (bf16[1,2048,128]{2,1,0:T(8,128)(2,1)S(1)}, bf16[1,2048,128]{2,1,0:T(8,128)(2,1)}, u32[]{:S(2)}) copy-start(bf16[1,2048,128]{2,1,0:T(8,128)(2,1)} %param.13) | copy-start | bytes 1572868
  253.2 14.6 %copy-start.7 = (f32[512,128]{1,0:T(8,128)}, f32[512,128]{1,0:T(8,128)S(1)}, u32[]{:S(2)}) copy-start(f32[512,128]{1,0:T(8,128)S(1)} %convolution_negate_fusion.1) | copy-start | bytes 786436
  301.3 7.0 %copy-start.6 = (bf16[1,2048,128]{2,1,0:T(8,128)(2,1)S(1)}, bf16[1,2048,128]{2,1,0:T(8,128)(2,1)}, u32[]{:S(2)}) copy-start(bf16[1,2048,128]{2,1,0:T(8,128)(2,1)} %param.17) | copy-start | bytes 1572868
  301.3 69.9 %all-to-all-start.1 = ((f32[16,512,128]{2,1,0:T(8,128)}), f32[16,512,128]{2,1,0:T(8,128)}, u32[]{:S(2)}, u32[]{:S(2)}) async-start(f32[16,512,128]{2,1,0:T(8,128)} %select_multiply_fusion), calls=%async_computation.1 | async-start | bytes 8388608 | tf_op jit(solution)/shard_map/all_to_all | solution.py:72
  375.5 6.2 copy-start.15
  375.5 6.3 %copy-start.10 = (bf16[1,512,128]{2,1,0:T(8,128)(2,1)S(1)}, bf16[1,512,128]{2,1,0:T(8,128)(2,1)}, u32[]{:S(2)}) copy-start(bf16[1,512,128]{2,1,0:T(8,128)(2,1)} %param.18) | copy-start | bytes 393220
  375.5 227.8 %all-to-all-start.2 = ((bf16[16,2048,128]{1,2,0:T(8,128)(2,1)}), bf16[16,2048,128]{1,2,0:T(8,128)(2,1)}, u32[]{:S(2)}, u32[]{:S(2)}) async-start(bf16[16,2048,128]{1,2,0:T(8,128)(2,1)} %stack.7), calls=%async_computation.2 | async-start | bytes 16777216 | tf_op jit(solution)/shard_map/all_to_all | solution.py:35
  381.6 97.5 %all-gather.9.cloned.1.call-start = ((), (), s32[]{:S(2)}) async-start(), calls=%async_computation.5 | async-start | bytes 2228224 | tf_op jit(solution)/shard_map/all_gather | solution.py:27
  382.6 209.4 %all-gather.11.cloned.1.call-start = ((), (), s32[]{:S(2)}) async-start(), calls=%async_computation.6 | async-start | bytes 4456448 | tf_op jit(solution)/shard_map/all_gather | solution.py:19
  482.8 117.2 %copy-start.3 = (bf16[512,2048]{1,0:T(8,128)(2,1)S(1)}, bf16[512,2048]{1,0:T(8,128)(2,1)}, u32[]{:S(2)}) copy-start(bf16[512,2048]{1,0:T(8,128)(2,1)} %all-gather.9.cloned.1.call-done) | copy-start | bytes 6291460
  600.0 14.7 %copy-start.8 = (f32[512,128]{1,0:T(8,128)}, f32[512,128]{1,0:T(8,128)S(1)}, u32[]{:S(2)}) copy-start(f32[512,128]{1,0:T(8,128)S(1)} %convolution_negate_fusion) | copy-start | bytes 786436
  603.3 12.7 %copy-start.1 = (f32[2048,128]{1,0:T(8,128)S(1)}, f32[2048,128]{1,0:T(8,128)}, u32[]{:S(2)}) copy-start(f32[2048,128]{1,0:T(8,128)} %param.12) | copy-start | bytes 3145732
Sparse Core Ops, SparseCore 0:
  26.2 94.7 all-gather.4
  123.3 116.2 all-gather.6
  384.8 94.3 all-gather.8
  481.4 110.4 all-gather.10
